TPU v7x, 32 devices: a whole 2x2x4 slice. The times are simulated.
32 devices in a mesh: groups: 2 (over y), attn: 4 (over x, core), exp: 4 (over z).
Axes of the slice: x: 2, y: 2, z: 4, core: 2. Of those that a mesh axis runs over, the one named last changes fastest.
Arguments:
- queries: bfloat16 [64, 32, 4096], P(('groups', 'exp'), None, 'attn'), parts along dimension 0, may hold values from -20 to 20
- new_keys: bfloat16 [64, 32, 512], P(('groups', 'exp'), None, 'attn'), parts along dimension 0, may hold values from -4 to 4
- new_values: bfloat16 [64, 32, 512], P(('groups', 'exp'), None, 'attn'), parts along dimension 0, may hold values from -4 to 4
- cache_keys: bfloat16 [64, 256, 512], P(('groups', 'exp'), None, 'attn'), parts along dimension 0, may hold values from -4 to 4
- cache_values: bfloat16 [64, 256, 512], P(('groups', 'exp'), None, 'attn'), parts along dimension 0, may hold values from -4 to 4
- cache_len: int32 [64], P(('groups', 'exp')), parts along dimension 0, may hold values from 2 to 256, as said below
- out_weight: bfloat16 [4096, 2048], P('attn', 'exp'), may hold values from -4 to 4
- residual: float32 [2048, 2048], P(('groups', 'exp', 'attn')), parts along dimension 0, may hold values from -6 to 6
- norm_gain: float32 [2048], replicated, may hold values from 0.1 to 1.9
- expert_ids: int32 [2048, 8], P(('groups', 'exp', 'attn')), parts along dimension 0, may hold values from 0 to 15, all different within a row; in each aligned block of 64 rows (0 to 63, 64 to 127, ...) at most 64 rows name the same one
- gate_nums: int32 [2048, 8], P(('groups', 'exp', 'attn')), parts along dimension 0, may hold values from 1 to 16
- w_gate_up: bfloat16 [16, 2048, 1536], P(('attn', 'exp')), may hold values from -0.125 to 0.125
- w_down: bfloat16 [16, 768, 2048], P(('attn', 'exp')), may hold values from -0.21875 to 0.21875
Outputs:
- mixed: float32 [2048, 2048], P(('groups', 'exp', 'attn')), parts along dimension 0
There are 2 independent parts, one for each index of `groups`. A program takes and returns all parts, laid end to end along the dimension named above; an argument that names none is the same for every part. Nothing has to cross between parts.
Inputs may be any that keep to these rules, and one draw needn't show every extreme that they name: `cache_len`: number of valid cache slots of each session; some session has all 256. `expert_ids`: within the 64 rows of one device, no expert is named by more than 64 rows, and this bound is reached; each row names 8 distinct experts.
All inputs are finite; a program needn't handle non-finite values.
Results may differ from a plain program's by a relative error of at most 0.0038.
Values may be sent and summed in bfloat16 or wider, within the bound.
A program may use at most 128 MiB of HBM per device.

v0:
```python
import jax
import jax.numpy as jnp
from jax import lax
from jax.sharding import PartitionSpec as P

HD = 128


def attend_session(packed):
    q_s, k_new, v_new, k_old, v_old, length = packed
    n_new = q_s.shape[0]
    n_old = k_old.shape[0]
    kv_count = k_old.shape[-1] // HD
    group_size = q_s.shape[-1] // (kv_count * HD)
    q_four = q_s.reshape(n_new, kv_count, group_size, HD)
    k_old3 = k_old.reshape(n_old, kv_count, HD)
    v_old3 = v_old.reshape(n_old, kv_count, HD)
    k_new3 = k_new.reshape(n_new, kv_count, HD)
    v_new3 = v_new.reshape(n_new, kv_count, HD)
    scale = 1.0 / HD**0.5
    s_old = jnp.einsum("ikgd,jkd->kgij", q_four, k_old3, preferred_element_type=jnp.float32) * scale
    s_new = jnp.einsum("ikgd,jkd->kgij", q_four, k_new3, preferred_element_type=jnp.float32) * scale
    valid_old = jnp.arange(n_old, dtype=jnp.int32) < length
    s_old = jnp.where(valid_old[None, None, None, :], s_old, jnp.float32(-1e30))
    causal = (
        jnp.arange(n_new, dtype=jnp.int32)[None, :] <= jnp.arange(n_new, dtype=jnp.int32)[:, None]
    )
    s_new = jnp.where(causal[None, None], s_new, jnp.float32(-1e30))
    top = jnp.maximum(jnp.max(s_old, -1, keepdims=True), jnp.max(s_new, -1, keepdims=True))
    e_old = jnp.exp(s_old - top)
    e_new = jnp.exp(s_new - top)
    total = jnp.sum(e_old, -1, keepdims=True) + jnp.sum(e_new, -1, keepdims=True)
    p_old = (e_old / total).astype(jnp.bfloat16)
    p_new = (e_new / total).astype(jnp.bfloat16)
    out = jnp.einsum("kgij,jkd->ikgd", p_old, v_old3, preferred_element_type=jnp.float32)
    out = out + jnp.einsum("kgij,jkd->ikgd", p_new, v_new3, preferred_element_type=jnp.float32)
    return out.reshape(n_new, kv_count * group_size * HD).astype(jnp.bfloat16)


def shards(
    queries,
    new_keys,
    new_values,
    cache_keys,
    cache_values,
    cache_len,
    out_weight,
    residual,
    norm_gain,
    expert_ids,
    gate_nums,
    w_gate_up,
    w_down,
):
    attended = lax.map(
        attend_session, (queries, new_keys, new_values, cache_keys, cache_values, cache_len)
    )
    local_rows = attended.reshape(attended.shape[0] * attended.shape[1], attended.shape[2])
    spread = jnp.dot(
        lax.all_gather(local_rows, "exp", axis=0, tiled=True),
        out_weight,
        preferred_element_type=jnp.float32,
    )
    partial_value = lax.all_to_all(spread, "exp", split_axis=0, concat_axis=1, tiled=True)
    projected = lax.psum_scatter(partial_value, "attn", scatter_dimension=0, tiled=True)
    middle = residual + projected
    meansq = jnp.mean(middle * middle, -1, keepdims=True)
    normed = (middle * lax.rsqrt(meansq + 1e-06) * norm_gain).astype(jnp.bfloat16)
    tok_rows = expert_ids.shape[0]
    top_count = expert_ids.shape[1]
    exp_dev = w_gate_up.shape[0]
    hidden_units = w_down.shape[1]
    n_experts = exp_dev * lax.axis_size("attn") * lax.axis_size("exp")
    capacity = max(2, 2 * tok_rows * top_count // n_experts)
    flat_ids = expert_ids.reshape(-1)
    onehot = (flat_ids[:, None] == jnp.arange(n_experts, dtype=jnp.int32)[None, :]).astype(
        jnp.int32
    )
    before = jnp.cumsum(onehot, axis=0) - onehot
    slot = jnp.sum(before * onehot, -1)
    target = (flat_ids * capacity + slot).reshape(tok_rows, top_count)
    places = jnp.arange(n_experts * capacity, dtype=jnp.int32)
    placing = jnp.sum((places[:, None, None] == target[None, :, :]).astype(jnp.int32), -1).astype(
        jnp.bfloat16
    )
    sent = jnp.dot(placing, normed, preferred_element_type=jnp.float32).astype(jnp.bfloat16)
    sent = sent.reshape(n_experts, capacity, normed.shape[1])
    block = lax.all_to_all(sent, ("attn", "exp"), split_axis=0, concat_axis=0, tiled=True)
    n_src = block.shape[0] // exp_dev
    rows_four = block.reshape(n_src, exp_dev, block.shape[1], block.shape[2])
    both = jnp.einsum("sjmd,jdf->sjmf", rows_four, w_gate_up, preferred_element_type=jnp.float32)
    hidden = (jax.nn.silu(both[..., :hidden_units]) * both[..., hidden_units:]).astype(jnp.bfloat16)
    result = jnp.einsum("sjmf,jfd->sjmd", hidden, w_down, preferred_element_type=jnp.float32)
    result = result.astype(jnp.bfloat16).reshape(block.shape)
    returned = lax.all_to_all(result, ("attn", "exp"), split_axis=0, concat_axis=0, tiled=True)
    picked = (
        returned[flat_ids, slot].reshape(tok_rows, top_count, normed.shape[1]).astype(jnp.float32)
    )
    numer = gate_nums.astype(jnp.float32)
    weights = numer / jnp.sum(numer, -1, keepdims=True)
    return middle + jnp.sum(picked * weights[:, :, None], 1)


def solution(mesh):
    in_specs = (
        P(("groups", "exp"), None, "attn"),
        P(("groups", "exp"), None, "attn"),
        P(("groups", "exp"), None, "attn"),
        P(("groups", "exp"), None, "attn"),
        P(("groups", "exp"), None, "attn"),
        P(("groups", "exp")),
        P("attn", "exp"),
        P(("groups", "exp", "attn"), None),
        P(),
        P(("groups", "exp", "attn"), None),
        P(("groups", "exp", "attn"), None),
        P(("attn", "exp"), None, None),
        P(("attn", "exp"), None, None),
    )
    out_specs = P(("groups", "exp", "attn"), None)
    return jax.shard_map(shards, mesh=mesh, in_specs=in_specs, out_specs=out_specs, check_vma=False)
```

profile of v0, /device:TPU:0, one launch (start us, length us, event | category | flops | bytes accessed | tf_op | source)
XLA Modules:
  0.0 444.1 jit_solution(16870406145571783817)
XLA Ops:
  6.5 63.9 %while.10 = (s32[]{:T(128)}, bf16[8,32,1024]{2,1,0:T(8,128)(2,1)}, bf16[8,256,128]{2,1,0:T(8,128)(2,1)}, s32[8]{0:T(128)}, bf16[8,256,128]{2,1,0:T(8,128)(2,1)},...) while((s32[]{:T(128)}, bf16[8,32,1024]{2,1,0:T(8,128)(2,1)}, ...), condition=%wide.region_5.6_spmd, body=%wide.region_0.5_spmd.sunk | while | flops 38404864 | bytes 2165389 | solution.py:55
  6.5 1.5 dynamic_slice.54
  8.7 0.9 dynamic-slice_bitcast_fusion.2
  9.6 0.9 fusion.71
  10.5 1.1 fusion.72
  11.9 0.9 fusion.75
  12.8 1.1 fusion.76
  14.7 1.3 dynamic_slice.54
  16.7 0.9 dynamic-slice_bitcast_fusion.2
  17.6 0.9 fusion.71
  18.5 1.1 fusion.72
  19.9 0.9 fusion.75
  20.8 1.1 fusion.76
  22.6 1.3 dynamic_slice.54
  24.7 0.9 dynamic-slice_bitcast_fusion.2
  25.5 0.9 fusion.71
  26.5 1.1 fusion.72
  27.9 0.9 fusion.75
  28.8 1.1 fusion.76
  30.6 1.3 dynamic_slice.54
  32.6 0.9 dynamic-slice_bitcast_fusion.2
  33.5 0.9 fusion.71
  34.4 1.1 fusion.72
  35.8 0.9 fusion.75
  36.7 1.1 fusion.76
  38.6 1.3 dynamic_slice.54
  40.6 0.9 dynamic-slice_bitcast_fusion.2
  41.5 0.9 fusion.71
  42.4 1.1 fusion.72
  43.8 0.9 fusion.75
  44.7 1.1 fusion.76
  46.6 1.3 dynamic_slice.54
  48.6 0.9 dynamic-slice_bitcast_fusion.2
  49.5 0.9 fusion.71
  50.4 1.1 fusion.72
  51.8 0.9 fusion.75
  52.7 1.1 fusion.76
  54.5 1.3 dynamic_slice.54
  57.4 0.9 fusion.71
  58.4 1.1 fusion.72
  59.8 0.9 fusion.75
  60.7 1.1 fusion.76
  62.5 1.3 dynamic_slice.54
  64.5 0.9 dynamic-slice_bitcast_fusion.2
  65.4 0.9 fusion.71
  66.3 1.1 fusion.72
  67.7 0.9 fusion.75
  68.6 1.1 fusion.76
  70.6 48.7 %all-gather.2.cloned.1.call-done = bf16[1024,1024]{1,0:T(8,128)(2,1)} async-done(((bf16[256,1024]{1,0:T(8,128)(2,1)}), bf16[1024,1024]{1,0:T(8,128)(2,1)}) %all-gather.2.cloned.1.call-update) | async-done | bytes 2097168 | tf_op jit(solution)/shard_map/all_gather | solution.py:60
  119.3 3.1 fusion.53
  122.4 50.9 %all_to_all.29 = f32[4,256,512]{2,1,0:T(8,128)S(1)} all-to-all(f32[4,256,512]{2,1,0:T(8,128)S(1)} %bitcast.131), channel_id=1, replica_groups=mesh['groups'=2,'attn'=4,'exp'=4] {'exp'}, dimensions={0} | all-to-all | bytes 4194304 | tf_op jit(solution)/shard_map/all_to_all | solution.py:64
  173.3 1.6 copy.56
  175.2 1.2 reduce-window.6
  177.7 27.8 %reduce-scatter.2.cloned.1.call-done = f32[64,2048]{1,0:T(8,128)} async-done(((f32[256,2048]{1,0:T(8,128)}), f32[64,2048]{1,0:T(8,128)}) %reduce-scatter.2.cloned.1.call-update) | async-done | bytes 524304 | tf_op jit(solution)/shard_map/reduce_scatter | solution.py:65
  205.5 1.4 multiply_reduce_fusion
  207.7 1.3 convolution_convert_fusion.1
  209.0 99.1 %all_to_all.30 = bf16[16,64,2048]{2,1,0:T(8,128)(2,1)S(1)} all-to-all(bf16[16,64,2048]{2,1,0:T(8,128)(2,1)S(1)} %bitcast.126), channel_id=1, replica_groups=mesh['groups'=2,'attn'=4,'exp'=4] {'attn','exp'}, dimensions={0} | all-to-all | bytes 8388608 | tf_op jit(solution)/shard_map/all_to_all | solution.py:88
  308.2 6.6 %fusion.30 = f32[16,1,64,1536]{3,2,0,1:T(8,128)S(1)} fusion(bf16[16,64,2048]{2,1,0:T(8,128)(2,1)S(1)} %all_to_all.30, bf16[1,2048,1536]{2,1,0:T(8,128)(2,1)S(1)} %bitcast.135), kind=kOutput, calls=%fused_computation.42 | convolution fusion | flops 6442450944 | bytes 16777216 | tf_op jit(solution)/shard_map/sjmd,jdf->sjmf/dot_general | solution.py:91
  314.8 5.1 %convolution_convert_fusion = bf16[16,64,2048]{2,1,0:T(8,128)(2,1)} fusion(bf16[1,768,2048]{2,1,0:T(8,128)(2,1)S(1)} %copy-done, f32[16,1,64,1536]{3,2,0,1:T(8,128)S(1)} %fusion.30), kind=kOutput, calls=%fused_computation.45 | convolution fusion | flops 3228041216 | bytes 13631488 | tf_op jit(solution)/shard_map/sjmf,jfd->sjmd/dot_general | solution.py:93
  319.9 4.8 %all-to-all-start.2 = ((bf16[16,64,2048]{2,1,0:T(8,128)(2,1)}), bf16[16,64,2048]{2,1,0:T(8,128)(2,1)}, u32[]{:S(2)}, u32[]{:S(2)}) async-start(bf16[16,64,2048]{2,1,0:T(8,128)(2,1)} %convolution_convert_fusion), calls=%async_computation.3 | async-start | bytes 8388608 | tf_op jit(solution)/shard_map/all_to_all | solution.py:95
  325.0 94.0 %all-to-all-done.2 = bf16[16,64,2048]{2,1,0:T(8,128)(2,1)} async-done(((bf16[16,64,2048]{2,1,0:T(8,128)(2,1)}), bf16[16,64,2048]{2,1,0:T(8,128)(2,1)}, u32[]{:S(2)}, u32[]{:S(2)}) %all-to-all-start.2) | async-done | bytes 4194336 | tf_op jit(solution)/shard_map/all_to_all | solution.py:95
  418.9 13.0 %gather_fusion = bf16[512,2048]{1,0:T(8,128)(2,1)} fusion(bf16[16,64,2048]{2,1,0:T(8,128)(2,1)} %all-to-all-done.2, s32[512]{0:T(512)S(1)} %bitcast.125), kind=kCustom, calls=%fused_computation | custom fusion | bytes 4198400 | tf_op jit(solution)/shard_map/gather | solution.py:97
  431.9 3.4 fusion.33
  435.4 1.9 add.75
  (120 shorter events, 16.8 us)
Async XLA Ops:
  6.5 308.3 %copy-start = (bf16[1,768,2048]{2,1,0:T(8,128)(2,1)S(1)}, bf16[1,768,2048]{2,1,0:T(8,128)(2,1)}, u32[]{:S(2)}) copy-start(bf16[1,768,2048]{2,1,0:T(8,128)(2,1)} %param.27) | copy-start | bytes 9437188
  6.5 112.8 %all-gather.2.cloned.1.call-start = ((), (), s32[]{:S(2)}) async-start(), calls=%async_computation.4 | async-start | bytes 2621440 | tf_op jit(solution)/shard_map/all_gather | solution.py:60
  70.5 135.0 %reduce-scatter.2.cloned.1.call-start = ((), (), s32[]{:S(2)}) async-start(), calls=%async_computation.5 | async-start | bytes 2621440 | tf_op jit(solution)/shard_map/reduce_scatter | solution.py:65
  173.3 1.6 copy-start.2
  174.9 32.8 %copy-start.4 = (f32[2048]{0:T(1024)S(1)}, f32[2048]{0:T(1024)}, u32[]{:S(2)}) copy-start(f32[2048]{0:T(1024)} %param.23) | copy-start | bytes 24580
  206.9 0.8 copy-start.1
  207.7 100.5 %slice-start = ((s8[6291456]{0:T(1024)(128)(4,1)}), s8[4194304]{0:T(1024)(128)(4,1)S(1)}, s32[]{:S(2)}) async-start(s8[6291456]{0:T(1024)(128)(4,1)} %bitcast.134), calls=%async_computation.6 | async-start | bytes 8388608
  209.0 99.1 %slice-start.1 = ((s8[6291456]{0:T(1024)(128)(4,1)}), s8[2097152]{0:T(1024)(128)(4,1)S(1)}, s32[]{:S(2)}) async-start(s8[6291456]{0:T(1024)(128)(4,1)} %bitcast.134), calls=%async_computation.7 | async-start | bytes 4194304
  319.9 4.9 %copy-start.3 = (s32[64,8]{0,1:T(8,128)S(1)}, s32[64,8]{0,1:T(8,128)}, u32[]{:S(2)}) copy-start(s32[64,8]{0,1:T(8,128)} %param.25) | copy-start | bytes 6148
  319.9 99.0 %all-to-all-start.2 = ((bf16[16,64,2048]{2,1,0:T(8,128)(2,1)}), bf16[16,64,2048]{2,1,0:T(8,128)(2,1)}, u32[]{:S(2)}, u32[]{:S(2)}) async-start(bf16[16,64,2048]{2,1,0:T(8,128)(2,1)} %convolution_convert_fusion), calls=%async_computation.3 | async-start | bytes 8388608 | tf_op jit(solution)/shard_map/all_to_all | solution.py:95
Sparse Core Ops, SparseCore 0:
  70.6 48.6 all-gather.1
  175.1 30.4 reduce-scatter.1
where the time goes:
time: 447 us; the launch traced here: 444 us
  waiting for transfers between devices  171 us (38%)
  blocking collectives  150 us (34%)
  matrix products  48.7 us (11%)
  local copies, waits for them, and re-layouts  39.5 us (9%)
  other arithmetic  16.3 us (4%)
  between operations  13.5 us (3%)
  starting transfers between devices  4.89 us (1%)
    all_to_all x1, blocking collectives, shards(): lax.all_to_all(sent, ('attn', 'exp'), split_axis=0, concat_axis=0, tiled=...  99.1 us
    all_to_all x1, waiting for transfers between devices, shards(): lax.all_to_all(result, ('attn', 'exp'), split_axis=0, concat_axis=0, tile...  94 us
    all_to_all x1, blocking collectives, shards(): lax.all_to_all(spread, 'exp', split_axis=0, concat_axis=1, tiled=True)  50.9 us
    all_gather x1, waiting for transfers between devices, shards(): lax.all_gather(local_rows, 'exp', axis=0, tiled=True)  48.7 us
    reduce_scatter x1, waiting for transfers between devices, shards(): lax.psum_scatter(partial_value, 'attn', scatter_dimension=0, tiled=True)  27.8 us
    gather x1, local copies, waits for them, and re-layouts, shards(): returned[flat_ids, slot].reshape(tok_rows, top_count, normed.shape[1])  13 us
    dynamic_slice x8, local copies, waits for them, and re-layouts, shards(): lax.map(attend_session, (queries, new_keys, new_values, cache_keys, cache...  10.7 us
  transfers between devices with their start and end apart: 3, of which 3 were waited for; matrix products, arithmetic and copies ran while one was open for 1% of the time, Pallas kernels for 0%

commit v1 on v0

--- a/solution.py
+++ b/solution.py
@@ -4,6 +4,28 @@
 from jax.sharding import PartitionSpec as P
 
 HD = 128
+
+
+def cut_along(x, dim, devices):
+    before, after = (x.shape[:dim], x.shape[dim + 1 :])
+    return jnp.moveaxis(x.reshape(*before, devices, -1, *after), dim, 0)
+
+
+def laid_out(tiles, dim):
+    tiles = jnp.moveaxis(tiles, 0, dim)
+    dims = tiles.shape
+    return tiles.reshape(*dims[:dim], dims[dim] * dims[dim + 1], *dims[dim + 2 :])
+
+
+def exchange_in_pairs(x, axis, split_dim, concat_dim):
+    size, index = (lax.axis_size(axis), lax.axis_index(axis))
+    blocks = cut_along(x, split_dim, size)
+    finished = [blocks[index]]
+    for turn in range(1, size):
+        sent = blocks[index ^ turn]
+        finished.append(lax.ppermute(sent, axis, [(i, i ^ turn) for i in range(size)]))
+    blocks = jnp.stack(finished)[index ^ jnp.arange(size)]
+    return laid_out(blocks, concat_dim)
 
 
 def attend_session(packed):
@@ -85,7 +107,7 @@
     )
     sent = jnp.dot(placing, normed, preferred_element_type=jnp.float32).astype(jnp.bfloat16)
     sent = sent.reshape(n_experts, capacity, normed.shape[1])
-    block = lax.all_to_all(sent, ("attn", "exp"), split_axis=0, concat_axis=0, tiled=True)
+    block = exchange_in_pairs(sent, ("attn", "exp"), 0, 0)
     n_src = block.shape[0] // exp_dev
     rows_four = block.reshape(n_src, exp_dev, block.shape[1], block.shape[2])
     both = jnp.einsum("sjmd,jdf->sjmf", rows_four, w_gate_up, preferred_element_type=jnp.float32)

time: 447 us -> 454 us (1.016)
  blocking collectives: 150 us -> 50.9 us
  starting transfers between devices: 4.89 us -> 52 us
  waiting for transfers between devices: 171 us -> 210 us
  local copies, waits for them, and re-layouts: 39.5 us -> 56.7 us
    all_to_all x1 -> x0, blocking collectives: 99.1 us -> none  [shards(): lax.all_to_all(sent, ('attn', 'exp'), split_axis=0, concat_axis=0, tiled=...]
    ppermute x0 -> x15, starting transfers between devices: none -> 41.4 us  [exchange_in_pairs(): lax.ppermute(sent, axis, [(i, i ^ turn) for i in range(size)])]
    ppermute x0 -> x15, waiting for transfers between devices: none -> 39 us  [exchange_in_pairs(): lax.ppermute(sent, axis, [(i, i ^ turn) for i in range(size)])]
    unnamed x15 -> x25, local copies, waits for them, and re-layouts: 0.89 us -> 11.1 us
    all_to_all x1, starting transfers between devices: 4.85 us -> 10.6 us  [shards(): lax.all_to_all(result, ('attn', 'exp'), split_axis=0, concat_axis=0, tile...]
    gather x0 -> x1, local copies, waits for them, and re-layouts: none -> 4.97 us  [exchange_in_pairs(): blocks = jnp.stack(finished)[index ^ jnp.arange(size)]]
  transfers between devices with their start and end apart: 3 -> 18, of which waited for: 3 -> 9; matrix products, arithmetic and copies ran while one was open for 1% -> 3% of each run, Pallas kernels for 0% -> 0%
where the time goes in v1:
time: 454 us; the launch traced here: 452 us
  waiting for transfers between devices  210 us (46%)
  local copies, waits for them, and re-layouts  56.7 us (12%)
  starting transfers between devices  52 us (11%)
  matrix products  52 us (11%)
  blocking collectives  50.9 us (11%)
  other arithmetic  16.3 us (4%)
  between operations  13.6 us (3%)
    all_to_all x1, waiting for transfers between devices, shards(): lax.all_to_all(result, ('attn', 'exp'), split_axis=0, concat_axis=0, tile...  94.2 us
    all_to_all x1, blocking collectives, shards(): lax.all_to_all(spread, 'exp', split_axis=0, concat_axis=1, tiled=True)  50.9 us
    all_gather x1, waiting for transfers between devices, shards(): lax.all_gather(local_rows, 'exp', axis=0, tiled=True)  48.7 us
    ppermute x15, starting transfers between devices, exchange_in_pairs(): lax.ppermute(sent, axis, [(i, i ^ turn) for i in range(size)])  41.4 us
    ppermute x15, waiting for transfers between devices, exchange_in_pairs(): lax.ppermute(sent, axis, [(i, i ^ turn) for i in range(size)])  39 us
    reduce_scatter x1, waiting for transfers between devices, shards(): lax.psum_scatter(partial_value, 'attn', scatter_dimension=0, tiled=True)  27.8 us
    gather x1, local copies, waits for them, and re-layouts, shards(): returned[flat_ids, slot].reshape(tok_rows, top_count, normed.shape[1])  13 us
    unnamed x25, local copies, waits for them, and re-layouts  11.1 us
  transfers between devices with their start and end apart: 18, of which 9 were waited for; matrix products, arithmetic and copies ran while one was open for 3% of the time, Pallas kernels for 0%

profile of v1, /device:TPU:0, one launch (start us, length us, event | category | flops | bytes accessed | tf_op | source)
XLA Modules:
  0.0 452.0 jit_solution(15842743970440035173)
XLA Ops:
  6.5 63.9 %while.10 = (s32[]{:T(128)}, bf16[8,32,1024]{2,1,0:T(8,128)(2,1)}, bf16[8,256,128]{2,1,0:T(8,128)(2,1)}, s32[8]{0:T(128)}, bf16[8,256,128]{2,1,0:T(8,128)(2,1)},...) while((s32[]{:T(128)}, bf16[8,32,1024]{2,1,0:T(8,128)(2,1)}, ...), condition=%wide.region_5.6_spmd, body=%wide.region_0.5_spmd.sunk | while | flops 38404864 | bytes 2167921 | solution.py:77
  6.5 1.0 dynamic-slice_bitcast_fusion.17
  7.6 1.3 dynamic_slice.134
  9.6 1.1 fusion.73
  10.7 0.9 fusion.72
  11.9 0.9 fusion.76
  12.8 1.1 fusion.77
  15.5 1.3 dynamic_slice.134
  17.5 1.1 fusion.73
  18.7 0.9 fusion.72
  19.9 0.9 fusion.76
  20.8 1.1 fusion.77
  23.5 1.3 dynamic_slice.134
  25.5 1.1 fusion.73
  26.7 0.9 fusion.72
  28.8 1.1 fusion.77
  31.5 1.3 dynamic_slice.134
  33.5 1.1 fusion.73
  34.6 0.9 fusion.72
  36.7 1.1 fusion.77
  39.4 1.3 dynamic_slice.134
  41.5 1.1 fusion.73
  42.6 0.9 fusion.72
  44.7 1.1 fusion.77
  47.4 1.3 dynamic_slice.134
  49.4 1.1 fusion.73
  50.6 0.9 fusion.72
  52.7 1.1 fusion.77
  55.4 1.3 dynamic_slice.134
  57.4 1.1 fusion.73
  58.5 0.9 fusion.72
  60.7 1.1 fusion.77
  63.4 1.3 dynamic_slice.134
  65.4 1.1 fusion.73
  66.5 0.9 fusion.72
  68.6 1.1 fusion.77
  70.6 48.7 %all-gather.2.cloned.1.call-done = bf16[1024,1024]{1,0:T(8,128)(2,1)} async-done(((bf16[256,1024]{1,0:T(8,128)(2,1)}), bf16[1024,1024]{1,0:T(8,128)(2,1)}) %all-gather.2.cloned.1.call-update) | async-done | bytes 2097168 | tf_op jit(solution)/shard_map/all_gather | solution.py:82
  119.3 3.1 fusion.54
  122.4 50.9 %all_to_all.24 = f32[4,256,512]{2,1,0:T(8,128)S(1)} all-to-all(f32[4,256,512]{2,1,0:T(8,128)S(1)} %bitcast.194), channel_id=1, replica_groups=mesh['groups'=2,'attn'=4,'exp'=4] {'exp'}, dimensions={0} | all-to-all | bytes 4194304 | tf_op jit(solution)/shard_map/all_to_all | solution.py:86
  173.3 1.6 copy.56
  175.3 1.2 reduce-window.6
  177.8 27.8 %reduce-scatter.2.cloned.1.call-done = f32[64,2048]{1,0:T(8,128)} async-done(((f32[256,2048]{1,0:T(8,128)}), f32[64,2048]{1,0:T(8,128)}) %reduce-scatter.2.cloned.1.call-update) | async-done | bytes 524304 | tf_op jit(solution)/shard_map/reduce_scatter | solution.py:87
  205.6 1.4 multiply_reduce_fusion
  207.8 1.3 convolution_convert_fusion.1
  209.1 1.3 dynamic-slice_bitcast_fusion.1
  210.4 1.5 collective-permute-start
  211.9 2.5 collective-permute-start.1
  215.6 8.8 %collective-permute-done = bf16[1,64,2048]{2,1,0:T(8,128)(2,1)S(1)} collective-permute-done((bf16[1,64,2048]{2,1,0:T(8,128)(2,1)S(1)}, bf16[1,64,2048]{2,1,0:T(8,128)(2,1)S(1)}, u32[]{:S(2)}, u32[]{:S(2)}) %collective-permute-start) | collective-permute-done | bytes 262176 | tf_op jit(solution)/shard_map/ppermute | solution.py:26
  225.1 8.3 %collective-permute-done.1 = bf16[1,64,2048]{2,1,0:T(8,128)(2,1)S(1)} collective-permute-done((bf16[1,64,2048]{2,1,0:T(8,128)(2,1)S(1)}, bf16[1,64,2048]{2,1,0:T(8,128)(2,1)S(1)}, u32[]{:S(2)}, u32[]{:S(2)}) %collective-permute-start.1) | collective-permute-done | bytes 262176 | tf_op jit(solution)/shard_map/ppermute | solution.py:26
  235.4 17.6 %collective-permute-start.8 = (bf16[1,64,2048]{2,1,0:T(8,128)(2,1)S(1)}, bf16[1,64,2048]{2,1,0:T(8,128)(2,1)S(1)}, u32[]{:S(2)}, u32[]{:S(2)}) collective-permute-start(bf16[1,64,2048]{2,1,0:T(8,128)(2,1)S(1)} %get-tuple-element.76), channel_id=1, source_target_pairs={{0,9},{1,8},{2,11},{3,10},{4,13},{5,12},{6,15},{7,14},{8,1},{9,0},... | collective-permute-start | bytes 786440 | tf_op jit(solution)/shard_map/ppermute | solution.py:26
  256.0 2.4 collective-permute-start.10
  259.1 3.7 collective-permute-start.11
  263.5 10.8 %collective-permute-start.12 = (bf16[1,64,2048]{2,1,0:T(8,128)(2,1)S(1)}, bf16[1,64,2048]{2,1,0:T(8,128)(2,1)S(1)}, u32[]{:S(2)}, u32[]{:S(2)}) collective-permute-start(bf16[1,64,2048]{2,1,0:T(8,128)(2,1)S(1)} %get-tuple-element.72), channel_id=1, source_target_pairs={{0,13},{1,12},{2,15},{3,14},{4,9},{5,8},{6,11},{7,10},{8,5},{9,4},... | collective-permute-start | bytes 786440 | tf_op jit(solution)/shard_map/ppermute | solution.py:26
  275.9 2.6 collective-permute-done.9
  280.0 8.4 %collective-permute-done.11 = bf16[1,64,2048]{2,1,0:T(8,128)(2,1)S(1)} collective-permute-done((bf16[1,64,2048]{2,1,0:T(8,128)(2,1)S(1)}, bf16[1,64,2048]{2,1,0:T(8,128)(2,1)S(1)}, u32[]{:S(2)}, u32[]{:S(2)}) %collective-permute-start.11) | collective-permute-done | bytes 262176 | tf_op jit(solution)/shard_map/ppermute | solution.py:26
  289.9 10.4 %collective-permute-done.13 = bf16[1,64,2048]{2,1,0:T(8,128)(2,1)S(1)} collective-permute-done((bf16[1,64,2048]{2,1,0:T(8,128)(2,1)S(1)}, bf16[1,64,2048]{2,1,0:T(8,128)(2,1)S(1)}, u32[]{:S(2)}, u32[]{:S(2)}) %collective-permute-start.13) | collective-permute-done | bytes 262176 | tf_op jit(solution)/shard_map/ppermute | solution.py:26
  301.8 5.0 %gather_fusion = bf16[16,64,2048]{2,1,0:T(8,128)(2,1)} fusion(bf16[16,64,2048]{2,1,0:T(8,128)(2,1)} %bitcast.52, s32[1024]{0:T(1024)S(1)} %pad_clamp_fusion), kind=kCustom, calls=%fused_computation | custom fusion | bytes 8388672 | tf_op jit(solution)/shard_map/gather | solution.py:27
  306.8 10.0 %fusion.30 = f32[16,1,64,1536]{3,2,0,1:T(8,128)S(1)} fusion(bf16[16,64,2048]{2,1,0:T(8,128)(2,1)} %gather_fusion, bf16[1,2048,1536]{2,1,0:T(8,128)(2,1)} %param.26), kind=kOutput, calls=%fused_computation.43 | convolution fusion | flops 6442450944 | bytes 16777216 | tf_op jit(solution)/shard_map/sjmd,jdf->sjmf/dot_general | solution.py:113
  316.8 5.0 %convolution_convert_fusion = bf16[16,64,2048]{2,1,0:T(8,128)(2,1)} fusion(bf16[1,768,2048]{2,1,0:T(8,128)(2,1)S(1)} %copy-done, f32[16,1,64,1536]{3,2,0,1:T(8,128)S(1)} %fusion.30), kind=kOutput, calls=%fused_computation.46 | convolution fusion | flops 3228041216 | bytes 13631488 | tf_op jit(solution)/shard_map/sjmf,jfd->sjmd/dot_general | solution.py:115
  321.8 10.6 %all-to-all-start.1 = ((bf16[16,64,2048]{2,1,0:T(8,128)(2,1)}), bf16[16,64,2048]{2,1,0:T(8,128)(2,1)}, u32[]{:S(2)}, u32[]{:S(2)}) async-start(bf16[16,64,2048]{2,1,0:T(8,128)(2,1)} %convolution_convert_fusion), calls=%async_computation.2 | async-start | bytes 8388608 | tf_op jit(solution)/shard_map/all_to_all | solution.py:117
  332.6 94.2 %all-to-all-done.1 = bf16[16,64,2048]{2,1,0:T(8,128)(2,1)} async-done(((bf16[16,64,2048]{2,1,0:T(8,128)(2,1)}), bf16[16,64,2048]{2,1,0:T(8,128)(2,1)}, u32[]{:S(2)}, u32[]{:S(2)}) %all-to-all-start.1) | async-done | bytes 4194336 | tf_op jit(solution)/shard_map/all_to_all | solution.py:117
  426.8 13.0 %gather_fusion.1 = bf16[512,2048]{1,0:T(8,128)(2,1)} fusion(bf16[16,64,2048]{2,1,0:T(8,128)(2,1)} %all-to-all-done.1, s32[512]{0:T(512)S(1)} %bitcast.188), kind=kCustom, calls=%fused_computation.1 | custom fusion | bytes 4198400 | tf_op jit(solution)/shard_map/gather | solution.py:119
  439.8 3.4 fusion.33
  443.3 1.9 add.154
  (163 shorter events, 41.7 us)
Async XLA Ops:
  6.5 310.2 %copy-start = (bf16[1,768,2048]{2,1,0:T(8,128)(2,1)S(1)}, bf16[1,768,2048]{2,1,0:T(8,128)(2,1)}, u32[]{:S(2)}) copy-start(bf16[1,768,2048]{2,1,0:T(8,128)(2,1)} %param.27) | copy-start | bytes 9437188
  6.5 112.8 %all-gather.2.cloned.1.call-start = ((), (), s32[]{:S(2)}) async-start(), calls=%async_computation.3 | async-start | bytes 2621440 | tf_op jit(solution)/shard_map/all_gather | solution.py:82
  70.5 135.1 %reduce-scatter.2.cloned.1.call-start = ((), (), s32[]{:S(2)}) async-start(), calls=%async_computation.4 | async-start | bytes 2621440 | tf_op jit(solution)/shard_map/reduce_scatter | solution.py:87
  173.3 1.7 copy-start.2
  173.3 34.4 %copy-start.4 = (f32[2048]{0:T(1024)S(1)}, f32[2048]{0:T(1024)}, u32[]{:S(2)}) copy-start(f32[2048]{0:T(1024)} %param.23) | copy-start | bytes 24580
  207.0 0.8 copy-start.1
  210.4 14.0 %collective-permute-start = (bf16[1,64,2048]{2,1,0:T(8,128)(2,1)S(1)}, bf16[1,64,2048]{2,1,0:T(8,128)(2,1)S(1)}, u32[]{:S(2)}, u32[]{:S(2)}) collective-permute-start(bf16[1,64,2048]{2,1,0:T(8,128)(2,1)S(1)} %get-tuple-element.84), channel_id=1, source_target_pairs={{0,1},{1,0},{2,3},{3,2},{4,5},{5,4},{6,7},{7,6},{8,9},{9,8},{10,11... | collective-permute-start | bytes 786440 | tf_op jit(solution)/shard_map/ppermute | solution.py:26
  211.9 21.5 %collective-permute-start.1 = (bf16[1,64,2048]{2,1,0:T(8,128)(2,1)S(1)}, bf16[1,64,2048]{2,1,0:T(8,128)(2,1)S(1)}, u32[]{:S(2)}, u32[]{:S(2)}) collective-permute-start(bf16[1,64,2048]{2,1,0:T(8,128)(2,1)S(1)} %get-tuple-element.83), channel_id=1, source_target_pairs={{0,2},{1,3},{2,0},{3,1},{4,6},{5,7},{6,4},{7,5},{8,10},{9,11},{10,... | collective-permute-start | bytes 786440 | tf_op jit(solution)/shard_map/ppermute | solution.py:26
  214.4 19.7 %collective-permute-start.2 = (bf16[1,64,2048]{2,1,0:T(8,128)(2,1)S(1)}, bf16[1,64,2048]{2,1,0:T(8,128)(2,1)S(1)}, u32[]{:S(2)}, u32[]{:S(2)}) collective-permute-start(bf16[1,64,2048]{2,1,0:T(8,128)(2,1)S(1)} %get-tuple-element.82), channel_id=1, source_target_pairs={{0,3},{1,2},{2,1},{3,0},{4,7},{5,6},{6,5},{7,4},{8,11},{9,10},{10,... | collective-permute-start | bytes 786440 | tf_op jit(solution)/shard_map/ppermute | solution.py:26
  214.9 20.5 %collective-permute-start.3 = (bf16[1,64,2048]{2,1,0:T(8,128)(2,1)S(1)}, bf16[1,64,2048]{2,1,0:T(8,128)(2,1)S(1)}, u32[]{:S(2)}, u32[]{:S(2)}) collective-permute-start(bf16[1,64,2048]{2,1,0:T(8,128)(2,1)S(1)} %get-tuple-element.81), channel_id=1, source_target_pairs={{0,4},{1,5},{2,6},{3,7},{4,0},{5,1},{6,2},{7,3},{8,12},{9,13},{10,... | collective-permute-start | bytes 786440 | tf_op jit(solution)/shard_map/ppermute | solution.py:26
  214.9 38.9 %collective-permute-start.4 = (bf16[1,64,2048]{2,1,0:T(8,128)(2,1)S(1)}, bf16[1,64,2048]{2,1,0:T(8,128)(2,1)S(1)}, u32[]{:S(2)}, u32[]{:S(2)}) collective-permute-start(bf16[1,64,2048]{2,1,0:T(8,128)(2,1)S(1)} %get-tuple-element.80), channel_id=1, source_target_pairs={{0,5},{1,4},{2,7},{3,6},{4,1},{5,0},{6,3},{7,2},{8,13},{9,12},{10,... | collective-permute-start | bytes 786440 | tf_op jit(solution)/shard_map/ppermute | solution.py:26
  224.4 31.6 %collective-permute-start.5 = (bf16[1,64,2048]{2,1,0:T(8,128)(2,1)S(1)}, bf16[1,64,2048]{2,1,0:T(8,128)(2,1)S(1)}, u32[]{:S(2)}, u32[]{:S(2)}) collective-permute-start(bf16[1,64,2048]{2,1,0:T(8,128)(2,1)S(1)} %get-tuple-element.79), channel_id=1, source_target_pairs={{0,6},{1,7},{2,4},{3,5},{4,2},{5,3},{6,0},{7,1},{8,14},{9,15},{10,... | collective-permute-start | bytes 786440 | tf_op jit(solution)/shard_map/ppermute | solution.py:26
  233.4 25.7 %collective-permute-start.6 = (bf16[1,64,2048]{2,1,0:T(8,128)(2,1)S(1)}, bf16[1,64,2048]{2,1,0:T(8,128)(2,1)S(1)}, u32[]{:S(2)}, u32[]{:S(2)}) collective-permute-start(bf16[1,64,2048]{2,1,0:T(8,128)(2,1)S(1)} %get-tuple-element.78), channel_id=1, source_target_pairs={{0,7},{1,6},{2,5},{3,4},{4,3},{5,2},{6,1},{7,0},{8,15},{9,14},{10,... | collective-permute-start | bytes 786440 | tf_op jit(solution)/shard_map/ppermute | solution.py:26
  234.1 29.4 %collective-permute-start.7 = (bf16[1,64,2048]{2,1,0:T(8,128)(2,1)S(1)}, bf16[1,64,2048]{2,1,0:T(8,128)(2,1)S(1)}, u32[]{:S(2)}, u32[]{:S(2)}) collective-permute-start(bf16[1,64,2048]{2,1,0:T(8,128)(2,1)S(1)} %get-tuple-element.77), channel_id=1, source_target_pairs={{0,8},{1,9},{2,10},{3,11},{4,12},{5,13},{6,14},{7,15},{8,0},{9,1},... | collective-permute-start | bytes 786440 | tf_op jit(solution)/shard_map/ppermute | solution.py:26
  235.4 39.6 %collective-permute-start.8 = (bf16[1,64,2048]{2,1,0:T(8,128)(2,1)S(1)}, bf16[1,64,2048]{2,1,0:T(8,128)(2,1)S(1)}, u32[]{:S(2)}, u32[]{:S(2)}) collective-permute-start(bf16[1,64,2048]{2,1,0:T(8,128)(2,1)S(1)} %get-tuple-element.76), channel_id=1, source_target_pairs={{0,9},{1,8},{2,11},{3,10},{4,13},{5,12},{6,15},{7,14},{8,1},{9,0},... | collective-permute-start | bytes 786440 | tf_op jit(solution)/shard_map/ppermute | solution.py:26
  253.8 24.6 %collective-permute-start.9 = (bf16[1,64,2048]{2,1,0:T(8,128)(2,1)S(1)}, bf16[1,64,2048]{2,1,0:T(8,128)(2,1)S(1)}, u32[]{:S(2)}, u32[]{:S(2)}) collective-permute-start(bf16[1,64,2048]{2,1,0:T(8,128)(2,1)S(1)} %get-tuple-element.75), channel_id=1, source_target_pairs={{0,10},{1,11},{2,8},{3,9},{4,14},{5,15},{6,12},{7,13},{8,2},{9,3},... | collective-permute-start | bytes 786440 | tf_op jit(solution)/shard_map/ppermute | solution.py:26
  256.0 23.3 %collective-permute-start.10 = (bf16[1,64,2048]{2,1,0:T(8,128)(2,1)S(1)}, bf16[1,64,2048]{2,1,0:T(8,128)(2,1)S(1)}, u32[]{:S(2)}, u32[]{:S(2)}) collective-permute-start(bf16[1,64,2048]{2,1,0:T(8,128)(2,1)S(1)} %get-tuple-element.74), channel_id=1, source_target_pairs={{0,11},{1,10},{2,9},{3,8},{4,15},{5,14},{6,13},{7,12},{8,3},{9,2},... | collective-permute-start | bytes 786440 | tf_op jit(solution)/shard_map/ppermute | solution.py:26
  259.1 29.4 %collective-permute-start.11 = (bf16[1,64,2048]{2,1,0:T(8,128)(2,1)S(1)}, bf16[1,64,2048]{2,1,0:T(8,128)(2,1)S(1)}, u32[]{:S(2)}, u32[]{:S(2)}) collective-permute-start(bf16[1,64,2048]{2,1,0:T(8,128)(2,1)S(1)} %get-tuple-element.73), channel_id=1, source_target_pairs={{0,12},{1,13},{2,14},{3,15},{4,8},{5,9},{6,10},{7,11},{8,4},{9,5},... | collective-permute-start | bytes 786440 | tf_op jit(solution)/shard_map/ppermute | solution.py:26
  263.5 25.7 %collective-permute-start.12 = (bf16[1,64,2048]{2,1,0:T(8,128)(2,1)S(1)}, bf16[1,64,2048]{2,1,0:T(8,128)(2,1)S(1)}, u32[]{:S(2)}, u32[]{:S(2)}) collective-permute-start(bf16[1,64,2048]{2,1,0:T(8,128)(2,1)S(1)} %get-tuple-element.72), channel_id=1, source_target_pairs={{0,13},{1,12},{2,15},{3,14},{4,9},{5,8},{6,11},{7,10},{8,5},{9,4},... | collective-permute-start | bytes 786440 | tf_op jit(solution)/shard_map/ppermute | solution.py:26
  275.0 25.3 %collective-permute-start.13 = (bf16[1,64,2048]{2,1,0:T(8,128)(2,1)S(1)}, bf16[1,64,2048]{2,1,0:T(8,128)(2,1)S(1)}, u32[]{:S(2)}, u32[]{:S(2)}) collective-permute-start(bf16[1,64,2048]{2,1,0:T(8,128)(2,1)S(1)} %get-tuple-element.71), channel_id=1, source_target_pairs={{0,14},{1,15},{2,12},{3,13},{4,10},{5,11},{6,8},{7,9},{8,6},{9,7},... | collective-permute-start | bytes 786440 | tf_op jit(solution)/shard_map/ppermute | solution.py:26
  278.4 22.6 %collective-permute-start.14 = (bf16[1,64,2048]{2,1,0:T(8,128)(2,1)S(1)}, bf16[1,64,2048]{2,1,0:T(8,128)(2,1)S(1)}, u32[]{:S(2)}, u32[]{:S(2)}) collective-permute-start(bf16[1,64,2048]{2,1,0:T(8,128)(2,1)S(1)} %get-tuple-element.70), channel_id=1, source_target_pairs={{0,15},{1,14},{2,13},{3,12},{4,11},{5,10},{6,9},{7,8},{8,7},{9,6},... | collective-permute-start | bytes 786440 | tf_op jit(solution)/shard_map/ppermute | solution.py:26
  321.8 10.7 %copy-start.3 = (s32[64,8]{0,1:T(8,128)S(1)}, s32[64,8]{0,1:T(8,128)}, u32[]{:S(2)}) copy-start(s32[64,8]{0,1:T(8,128)} %param.25) | copy-start | bytes 6148
  321.8 105.0 %all-to-all-start.1 = ((bf16[16,64,2048]{2,1,0:T(8,128)(2,1)}), bf16[16,64,2048]{2,1,0:T(8,128)(2,1)}, u32[]{:S(2)}, u32[]{:S(2)}) async-start(bf16[16,64,2048]{2,1,0:T(8,128)(2,1)} %convolution_convert_fusion), calls=%async_computation.2 | async-start | bytes 8388608 | tf_op jit(solution)/shard_map/all_to_all | solution.py:117
Sparse Core Ops, SparseCore 0:
  70.6 48.6 all-gather.1
  175.1 30.4 reduce-scatter.1
